TPU v7x, 32 devices: a whole 2x2x4 slice. The times are simulated.
32 devices in a mesh: dp: 4 (over y, x), expert: 8 (over z, core).
Axes of the slice: x: 2, y: 2, z: 4, core: 2. Of those that a mesh axis runs over, the one named last changes fastest.
Arguments:
- tokens: bfloat16 [4096, 1536], P(('dp', 'expert')), may hold values from -6 to 6
- grad_out: bfloat16 [4096, 1536], P(('dp', 'expert')), may hold values from -6 to 6
- expert_ids: int32 [4096, 4], P(('dp', 'expert')), may hold values from 0 to 7, all different within a row; in each aligned block of 128 rows (0 to 127, 128 to 255, ...) at most 96 rows name the same one
- gate_q: int32 [4096, 4], P(('dp', 'expert')), may hold values from 1 to 65535
- w_up: bfloat16 [8, 1536, 768], P('expert', 'dp'), may hold values from -0.15625 to 0.15625
- w_down: bfloat16 [8, 768, 1536], P('expert', None, 'dp'), may hold values from -0.21875 to 0.21875
Outputs:
- dw_up: bfloat16 [8, 1536, 768], P('expert', 'dp')
- dw_down: bfloat16 [8, 768, 1536], P('expert', None, 'dp')
Inputs may be any that keep to these rules, and one draw needn't show every extreme that they name: `expert_ids`: within the rows of one device no expert is named by more than 96 rows, a bound that some block reaches; the 4 ids of a row differ.
All inputs are finite; a program needn't handle non-finite values.
Results may differ from a plain program's by a relative error of at most 0.0064.
Values may be sent and summed in bfloat16 or wider, within the bound.
No kernel may reach another device: no remote copies, remote signals or barrier semaphores. Data moves between devices by JAX's collectives and lax.ppermute only.
A program may use at most 64 MiB of HBM per device.

v0:
```python
import jax
import jax.numpy as jnp
from jax import lax
from jax.sharding import PartitionSpec as P


def silu_slope(values):
    sigmoid_part = jax.nn.sigmoid(values)
    return sigmoid_part * (1.0 + values * (1.0 - sigmoid_part))


def summed_up(recv_rows, projected_grad):
    first_dims = (((0,), (0,)), ((), ()))
    partial_value = lax.dot_general(
        recv_rows, projected_grad, first_dims, preferred_element_type=jnp.float32
    ).astype(jnp.bfloat16)
    pieces = lax.all_to_all(partial_value[None], "dp", split_axis=1, concat_axis=0, tiled=True)
    return jnp.sum(pieces.astype(jnp.float32), axis=0, keepdims=True).astype(jnp.bfloat16)


def summed_down(activated, grad_rows):
    first_dims = (((0,), (0,)), ((), ()))
    partial_value = lax.dot_general(
        activated, grad_rows, first_dims, preferred_element_type=jnp.float32
    ).astype(jnp.bfloat16)
    pieces = lax.all_to_all(partial_value[None], "dp", split_axis=2, concat_axis=0, tiled=True)
    return jnp.sum(pieces.astype(jnp.float32), axis=0, keepdims=True).astype(jnp.bfloat16)


def shards(tokens, grad_out, expert_ids, gate_q, w_up, w_down):
    devices = lax.axis_size("expert")
    token_count, top_count = expert_ids.shape
    model_width = tokens.shape[1]
    capacity = max(2, token_count * top_count * 3 // (2 * devices))
    slot_expert = expert_ids.reshape(-1)
    onehot_table = (slot_expert[:, None] == jnp.arange(devices, dtype=jnp.int32)[None, :]).astype(
        jnp.int32
    )
    earlier = jnp.cumsum(onehot_table, axis=0) - onehot_table
    slot_rank = jnp.sum(earlier * onehot_table, axis=1)
    slot_target = slot_expert * capacity + slot_rank
    gate_values = gate_q.reshape(-1).astype(jnp.float32) * (1.0 / 65536.0)
    token_rows = jnp.repeat(tokens, top_count, axis=0)
    slot_grads = (
        gate_values[:, None] * jnp.repeat(grad_out, top_count, axis=0).astype(jnp.float32)
    ).astype(jnp.bfloat16)
    empty_rows = jnp.zeros((devices * capacity, model_width), jnp.bfloat16)
    send_tokens = empty_rows.at[slot_target].set(token_rows).reshape(devices, capacity, model_width)
    grad_slots = empty_rows.at[slot_target].set(slot_grads).reshape(devices, capacity, model_width)
    contract_last = (((1,), (1,)), ((), ()))
    up_whole = lax.all_gather(w_up, "dp", axis=1, tiled=True)[0]
    down_whole = lax.all_gather(w_down, "dp", axis=2, tiled=True)[0]
    recv_tokens = lax.all_to_all(send_tokens, "expert", split_axis=0, concat_axis=0, tiled=True)
    recv_rows = recv_tokens.reshape(-1, model_width)
    projected = jnp.dot(recv_rows, up_whole, preferred_element_type=jnp.float32)
    recv_grads = lax.all_to_all(grad_slots, "expert", split_axis=0, concat_axis=0, tiled=True)
    activated = jax.nn.silu(projected).astype(jnp.bfloat16)
    grad_rows = recv_grads.reshape(-1, model_width)
    act_grad = lax.dot_general(
        grad_rows, down_whole, contract_last, preferred_element_type=jnp.float32
    )
    projected_grad = (act_grad * silu_slope(projected)).astype(jnp.bfloat16)
    up_grad = summed_up(recv_rows, projected_grad)
    down_grad = summed_down(activated, grad_rows)
    return (up_grad, down_grad)


def solution(mesh):
    in_specs = (
        P(("dp", "expert"), None),
        P(("dp", "expert"), None),
        P(("dp", "expert"), None),
        P(("dp", "expert"), None),
        P("expert", "dp", None),
        P("expert", None, "dp"),
    )
    out_specs = (P("expert", "dp", None), P("expert", None, "dp"))
    return jax.shard_map(shards, mesh=mesh, in_specs=in_specs, out_specs=out_specs, check_vma=False)
```

profile of v0, /device:TPU:0, one launch (start us, length us, event | category | flops | bytes accessed | tf_op | source)
XLA Modules:
  0.0 307.0 jit_solution(6901323254794781142)
XLA Ops:
  12.4 4.7 %scatter_custom_fusion = bf16[768,1536]{1,0:T(8,128)(2,1)} fusion(s32[512]{0:T(512)S(1)} %bitcast.53, bf16[512,1536]{1,0:T(8,128)(2,1)S(1)} %reshape.112, bf16[]{:T(256)} %constant.7.clone.1), kind=kCustom, calls=%fused_computation.18 | custom fusion | bytes 2359298 | tf_op jit(solution)/shard_map/scatter | solution.py:48
  17.1 6.5 %all-to-all-start = ((bf16[8,96,1536]{2,1,0:T(8,128)(2,1)}), bf16[8,96,1536]{2,1,0:T(8,128)(2,1)}, u32[]{:S(2)}, u32[]{:S(2)}) async-start(bf16[8,96,1536]{2,1,0:T(8,128)(2,1)} %bitcast.4), calls=%async_computation | async-start | bytes 4718592 | tf_op jit(solution)/shard_map/all_to_all | solution.py:53
  24.7 2.3 convert_element_type.78
  27.2 6.0 %scatter_custom_fusion.1 = bf16[768,1536]{1,0:T(8,128)(2,1)} fusion(s32[512]{0:T(512)S(1)} %bitcast.54, f32[512,1536]{1,0:T(8,128)} %convert_element_type.78, f32[512]{0:T(512)S(1)} %mul.59, bf16[]{:T(256)} %constant.7.clone.1), kind=kCustom, calls=%fused_computation.14 | custom fusion | flops 1572864 | bytes 5507074 | tf_op jit(solution)/shard_map/scatter | solution.py:49
  33.3 45.1 %all-to-all-done = bf16[8,96,1536]{2,1,0:T(8,128)(2,1)} async-done(((bf16[8,96,1536]{2,1,0:T(8,128)(2,1)}), bf16[8,96,1536]{2,1,0:T(8,128)(2,1)}, u32[]{:S(2)}, u32[]{:S(2)}) %all-to-all-start) | async-done | bytes 2359328 | tf_op jit(solution)/shard_map/all_to_all | solution.py:53
  78.3 3.6 %all-to-all-start.1 = ((bf16[8,96,1536]{2,1,0:T(8,128)(2,1)}), bf16[8,96,1536]{2,1,0:T(8,128)(2,1)S(1)}, u32[]{:S(2)}, u32[]{:S(2)}) async-start(bf16[8,96,1536]{2,1,0:T(8,128)(2,1)} %bitcast.6), calls=%async_computation.1 | async-start | bytes 4718592 | tf_op jit(solution)/shard_map/all_to_all | solution.py:56
  82.7 5.8 %fusion.2 = f32[768,768]{1,0:T(8,128)} fusion(bf16[768,1536]{1,0:T(8,128)(2,1)} %bitcast.5, bf16[1,1536,768]{2,1,0:T(8,128)(2,1)} %all-gather.5.cloned.1.call-done), kind=kOutput, calls=%fused_computation.7 | convolution fusion | flops 1811939328 | bytes 7077888 | tf_op jit(solution)/shard_map/dot_general | solution.py:55
  88.5 34.7 %all-gather.3.cloned.1.call-done = bf16[1,768,1536]{2,1,0:T(8,128)(2,1)} async-done(((bf16[1,768,384]{2,1,0:T(8,128)(2,1)}), bf16[1,768,1536]{2,1,0:T(8,128)(2,1)}) %all-gather.3.cloned.1.call-update) | async-done | bytes 2359312 | tf_op jit(solution)/shard_map/all_gather | solution.py:52
  123.2 13.3 %all-to-all-done.1 = bf16[8,96,1536]{2,1,0:T(8,128)(2,1)S(1)} async-done(((bf16[8,96,1536]{2,1,0:T(8,128)(2,1)}), bf16[8,96,1536]{2,1,0:T(8,128)(2,1)S(1)}, u32[]{:S(2)}, u32[]{:S(2)}) %all-to-all-start.1) | async-done | bytes 2359328 | tf_op jit(solution)/shard_map/all_to_all | solution.py:56
  137.9 8.2 %fusion = bf16[1,1536,768]{2,1,0:T(8,128)(2,1)S(1)} fusion(bf16[768,1536]{1,0:T(8,128)(2,1)} %bitcast.5, f32[768,768]{1,0:T(8,128)} %fusion.2, bf16[768,1536]{1,0:T(8,128)(2,1)} %bitcast.48, bf16[1,768,1536]{2,1,0:T(8,128)(2,1)} %all-gather.3.cloned.1.call-done), kind=kOutput, calls=%fused_computation.5 | convolution fusion | flops 3630366720 | bytes 11796480 | tf_op jit(solution)/shard_map/dot_general | solution.py:14
  146.1 33.8 %copy.34 = bf16[1,1536,768]{2,0,1:T(2,128)(2,1)} copy(bf16[1,1536,768]{2,1,0:T(8,128)(2,1)S(1)} %fusion) | data formatting | bytes 4718592 | tf_op jit(solution)/shard_map/broadcast_in_dim | solution.py:17
  180.4 24.1 %reduce.7 = bf16[1536,768]{1,0:T(8,128)(2,1)S(1)} reduce(bf16[1536,1,768]{2,1,0:T(2,128)(2,1)} %bitcast.42, bf16[]{:T(256)} %broadcast.72), dimensions={1}, to_apply=%bitcast.41.reduce_sub_computation | reduce | bytes 4718594
  204.5 2.3 reshape.129
  206.8 3.9 %all-to-all-start.2 = ((bf16[4,2,147456]{2,1,0:T(2,128)(2,1)}), bf16[4,2,147456]{2,1,0:T(2,128)(2,1)S(1)}, u32[]{:S(2)}, u32[]{:S(2)}) async-start(bf16[4,2,147456]{2,1,0:T(2,128)(2,1)} %reshape.129), calls=%async_computation.2 | async-start | bytes 4718592 | tf_op jit(solution)/shard_map/all_to_all | solution.py:17
  210.6 5.9 %fusion.1 = bf16[1,768,1536]{2,1,0:T(8,128)(2,1)} fusion(bf16[768,1536]{1,0:T(8,128)(2,1)} %bitcast.49, f32[768,768]{1,0:T(8,128)} %fusion.2), kind=kOutput, calls=%fused_computation.6 | convolution fusion | flops 1816068096 | bytes 7077888 | tf_op jit(solution)/shard_map/dot_general | solution.py:23
  216.5 12.1 %copy.29 = bf16[1,768,1536]{1,0,2:T(2,128)(2,1)} copy(bf16[1,768,1536]{2,1,0:T(8,128)(2,1)} %fusion.1) | data formatting | bytes 4718592 | tf_op jit(solution)/shard_map/broadcast_in_dim | solution.py:26
  228.6 25.5 %reduce.8 = bf16[1536,768]{1,0:T(8,128)(2,1)} reduce(bf16[1536,1,768]{2,1,0:T(2,128)(2,1)} %bitcast.43, bf16[]{:T(256)} %broadcast.72), dimensions={1}, to_apply=%bitcast.34.reduce_sub_computation | reduce | bytes 4718594
  254.1 4.1 %reshape.131 = bf16[4,2,147456]{2,1,0:T(2,128)(2,1)} reshape(bf16[1536,768]{1,0:T(8,128)(2,1)} %reduce.8) | data formatting | bytes 4718592
  258.2 4.5 %all-to-all-start.3 = ((bf16[4,2,147456]{2,1,0:T(2,128)(2,1)}), bf16[4,2,147456]{2,1,0:T(2,128)(2,1)}, u32[]{:S(2)}, u32[]{:S(2)}) async-start(bf16[4,2,147456]{2,1,0:T(2,128)(2,1)} %reshape.131), calls=%async_computation.3 | async-start | bytes 4718592 | tf_op jit(solution)/shard_map/all_to_all | solution.py:26
  262.7 3.6 %reshape.130 = bf16[1536,1,768]{2,1,0:T(2,128)(2,1)} reshape(bf16[4,2,147456]{2,1,0:T(2,128)(2,1)S(1)} %all-to-all-done.2) | data formatting | bytes 4718592
  266.3 2.7 copy.31
  270.3 20.1 %all-to-all-done.3 = bf16[4,2,147456]{2,1,0:T(2,128)(2,1)} async-done(((bf16[4,2,147456]{2,1,0:T(2,128)(2,1)}), bf16[4,2,147456]{2,1,0:T(2,128)(2,1)}, u32[]{:S(2)}, u32[]{:S(2)}) %all-to-all-start.3) | async-done | bytes 2359328 | tf_op jit(solution)/shard_map/all_to_all | solution.py:26
  290.5 5.2 %reshape.132 = bf16[1536,1,768]{2,1,0:T(2,128)(2,1)} reshape(bf16[4,2,147456]{2,1,0:T(2,128)(2,1)} %all-to-all-done.3) | data formatting | bytes 4718592
  295.6 2.7 copy.32
  (35 shorter events, 12.3 us)
Async XLA Ops:
  17.1 7.2 %copy-start.1 = (bf16[128,1536]{1,0:T(8,128)(2,1)S(1)}, bf16[128,1536]{1,0:T(8,128)(2,1)}, u32[]{:S(2)}) copy-start(bf16[128,1536]{1,0:T(8,128)(2,1)} %param.7) | copy-start | bytes 1179652
  17.1 61.2 %all-to-all-start = ((bf16[8,96,1536]{2,1,0:T(8,128)(2,1)}), bf16[8,96,1536]{2,1,0:T(8,128)(2,1)}, u32[]{:S(2)}, u32[]{:S(2)}) async-start(bf16[8,96,1536]{2,1,0:T(8,128)(2,1)} %bitcast.4), calls=%async_computation | async-start | bytes 4718592 | tf_op jit(solution)/shard_map/all_to_all | solution.py:53
  23.6 59.2 %all-gather.5.cloned.1.call-start = ((), (), s32[]{:S(2)}) async-start(), calls=%async_computation.5 | async-start | bytes 2949120 | tf_op jit(solution)/shard_map/all_gather | solution.py:51
  24.7 2.3 copy-start.2
  78.3 58.2 %all-to-all-start.1 = ((bf16[8,96,1536]{2,1,0:T(8,128)(2,1)}), bf16[8,96,1536]{2,1,0:T(8,128)(2,1)S(1)}, u32[]{:S(2)}, u32[]{:S(2)}) async-start(bf16[8,96,1536]{2,1,0:T(8,128)(2,1)} %bitcast.6), calls=%async_computation.1 | async-start | bytes 4718592 | tf_op jit(solution)/shard_map/all_to_all | solution.py:56
  81.9 41.3 %all-gather.3.cloned.1.call-start = ((), (), s32[]{:S(2)}) async-start(), calls=%async_computation.4 | async-start | bytes 2949120 | tf_op jit(solution)/shard_map/all_gather | solution.py:52
  136.5 1.4 copy-start
  206.8 51.5 %all-to-all-start.2 = ((bf16[4,2,147456]{2,1,0:T(2,128)(2,1)}), bf16[4,2,147456]{2,1,0:T(2,128)(2,1)S(1)}, u32[]{:S(2)}, u32[]{:S(2)}) async-start(bf16[4,2,147456]{2,1,0:T(2,128)(2,1)} %reshape.129), calls=%async_computation.2 | async-start | bytes 4718592 | tf_op jit(solution)/shard_map/all_to_all | solution.py:17
  258.2 32.2 %all-to-all-start.3 = ((bf16[4,2,147456]{2,1,0:T(2,128)(2,1)}), bf16[4,2,147456]{2,1,0:T(2,128)(2,1)}, u32[]{:S(2)}, u32[]{:S(2)}) async-start(bf16[4,2,147456]{2,1,0:T(2,128)(2,1)} %reshape.131), calls=%async_computation.3 | async-start | bytes 4718592 | tf_op jit(solution)/shard_map/all_to_all | solution.py:26
Sparse Core Ops, SparseCore 0:
  26.2 38.7 all-gather.4
  84.6 38.5 all-gather.2
where the time goes:
time: 308 us; the launch traced here: 307 us
  waiting for transfers between devices  114 us (37%)
  local copies, waits for them, and re-layouts  80.2 us (26%)
  other arithmetic  59.7 us (19%)
  matrix products  19.9 us (6%)
  starting transfers between devices  18.7 us (6%)
  between operations  14.2 us (5%)
    unnamed x2, other arithmetic  49.6 us
    all_to_all x1, waiting for transfers between devices, shards(): lax.all_to_all(send_tokens, 'expert', split_axis=0, concat_axis=0, tiled=...  45.1 us
    all_gather x1, waiting for transfers between devices, shards(): down_whole = lax.all_gather(w_down, 'dp', axis=2, tiled=True)[0]  34.7 us
    broadcast_in_dim x1, local copies, waits for them, and re-layouts, summed_up(): partial_value[None]  33.8 us
    unnamed x15, local copies, waits for them, and re-layouts  24.3 us
    all_to_all x1, waiting for transfers between devices, summed_down(): lax.all_to_all(partial_value[None], 'dp', split_axis=2, concat_axis=0, ti...  20.1 us
    all_to_all x1, waiting for transfers between devices, shards(): lax.all_to_all(grad_slots, 'expert', split_axis=0, concat_axis=0, tiled=T...  13.3 us
    broadcast_in_dim x1, local copies, waits for them, and re-layouts, summed_down(): partial_value[None]  12.1 us
  transfers between devices with their start and end apart: 6, of which 4 were waited for; matrix products, arithmetic and copies ran while one was open for 23% of the time, Pallas kernels for 0%

commit v1 on v0

--- a/solution.py
+++ b/solution.py
@@ -23,7 +23,12 @@
     partial_value = lax.dot_general(
         activated, grad_rows, first_dims, preferred_element_type=jnp.float32
     ).astype(jnp.bfloat16)
-    pieces = lax.all_to_all(partial_value[None], "dp", split_axis=2, concat_axis=0, tiled=True)
+    pieces = jnp.concatenate(
+        lax.all_to_all(
+            jnp.stack(jnp.split(partial_value[None], lax.axis_size("dp"), axis=2)), "dp", 0, 0
+        ),
+        axis=0,
+    )
     return jnp.sum(pieces.astype(jnp.float32), axis=0, keepdims=True).astype(jnp.bfloat16)
 
 

time: 308 us -> 280 us (0.909)
  local copies, waits for them, and re-layouts: 80.2 us -> 55.3 us
  other arithmetic: 59.7 us -> 38.3 us
  waiting for transfers between devices: 114 us -> 135 us
    unnamed x2 -> x1, other arithmetic: 49.6 us -> 24.1 us
    all_to_all x1, waiting for transfers between devices: 0.01 us -> 21 us  [summed_up(): lax.all_to_all(partial_value[None], 'dp', split_axis=1, concat_axis=0, ti...]
    unnamed x15 -> x11, local copies, waits for them, and re-layouts: 24.3 us -> 11.2 us
    broadcast_in_dim x1 -> x0, local copies, waits for them, and re-layouts: 12.1 us -> none  [summed_down(): partial_value[None]]
  transfers between devices with their start and end apart: 6 -> 6, of which waited for: 4 -> 5; matrix products, arithmetic and copies ran while one was open for 23% -> 10% of each run, Pallas kernels for 0% -> 0%
where the time goes in v1:
time: 280 us
  waiting for transfers between devices  135 us (48%)
  local copies, waits for them, and re-layouts  55.3 us (20%)
  other arithmetic  38.3 us (14%)
  starting transfers between devices  18.6 us (7%)
  matrix products  18.4 us (7%)
  between operations  14.2 us (5%)
    all_to_all x1, waiting for transfers between devices, shards(): lax.all_to_all(send_tokens, 'expert', split_axis=0, concat_axis=0, tiled=...  45.1 us
    all_gather x1, waiting for transfers between devices, shards(): down_whole = lax.all_gather(w_down, 'dp', axis=2, tiled=True)[0]  34.7 us
    broadcast_in_dim x1, local copies, waits for them, and re-layouts, summed_up(): partial_value[None]  33.8 us
    unnamed x1, other arithmetic  24.1 us
    all_to_all x1, waiting for transfers between devices, summed_up(): lax.all_to_all(partial_value[None], 'dp', split_axis=1, concat_axis=0, ti...  21 us
    all_to_all x1, waiting for transfers between devices, summed_down(): lax.all_to_all(jnp.stack(jnp.split(partial_value[None], lax.axis_size('dp...  19.6 us
    all_to_all x1, waiting for transfers between devices, shards(): lax.all_to_all(grad_slots, 'expert', split_axis=0, concat_axis=0, tiled=T...  13.3 us
    unnamed x11, local copies, waits for them, and re-layouts  11.2 us
  transfers between devices with their start and end apart: 6, of which 5 were waited for; matrix products, arithmetic and copies ran while one was open for 10% of the time, Pallas kernels for 0%

profile of v1, /device:TPU:0, one launch (start us, length us, event | category | flops | bytes accessed | tf_op | source)
XLA Modules:
  0.0 279.6 jit_solution(2208196081923102020)
XLA Ops:
  10.5 1.4 broadcast_in_dim.22
  12.4 4.7 %scatter_custom_fusion = bf16[768,1536]{1,0:T(8,128)(2,1)} fusion(s32[512]{0:T(512)S(1)} %bitcast.55, bf16[512,1536]{1,0:T(8,128)(2,1)S(1)} %reshape.112, bf16[]{:T(256)} %constant.7.clone.1), kind=kCustom, calls=%fused_computation.19 | custom fusion | bytes 2359298 | tf_op jit(solution)/shard_map/scatter | solution.py:53
  17.1 6.5 %all-to-all-start = ((bf16[8,96,1536]{2,1,0:T(8,128)(2,1)}), bf16[8,96,1536]{2,1,0:T(8,128)(2,1)}, u32[]{:S(2)}, u32[]{:S(2)}) async-start(bf16[8,96,1536]{2,1,0:T(8,128)(2,1)} %bitcast.4), calls=%async_computation | async-start | bytes 4718592 | tf_op jit(solution)/shard_map/all_to_all | solution.py:58
  24.8 2.3 convert_element_type.78
  27.2 6.0 %scatter_custom_fusion.1 = bf16[768,1536]{1,0:T(8,128)(2,1)} fusion(s32[512]{0:T(512)S(1)} %bitcast.56, f32[512,1536]{1,0:T(8,128)} %convert_element_type.78, f32[512]{0:T(512)S(1)} %mul.59, bf16[]{:T(256)} %constant.7.clone.1), kind=kCustom, calls=%fused_computation.15 | custom fusion | flops 1572864 | bytes 5507074 | tf_op jit(solution)/shard_map/scatter | solution.py:54
  33.3 45.1 %all-to-all-done = bf16[8,96,1536]{2,1,0:T(8,128)(2,1)} async-done(((bf16[8,96,1536]{2,1,0:T(8,128)(2,1)}), bf16[8,96,1536]{2,1,0:T(8,128)(2,1)}, u32[]{:S(2)}, u32[]{:S(2)}) %all-to-all-start) | async-done | bytes 2359328 | tf_op jit(solution)/shard_map/all_to_all | solution.py:58
  78.3 3.6 %all-to-all-start.1 = ((bf16[8,96,1536]{2,1,0:T(8,128)(2,1)}), bf16[8,96,1536]{2,1,0:T(8,128)(2,1)S(1)}, u32[]{:S(2)}, u32[]{:S(2)}) async-start(bf16[8,96,1536]{2,1,0:T(8,128)(2,1)} %bitcast.6), calls=%async_computation.1 | async-start | bytes 4718592 | tf_op jit(solution)/shard_map/all_to_all | solution.py:61
  82.7 5.8 %fusion.2 = f32[768,768]{1,0:T(8,128)} fusion(bf16[768,1536]{1,0:T(8,128)(2,1)} %bitcast.5, bf16[1,1536,768]{2,1,0:T(8,128)(2,1)} %all-gather.5.cloned.1.call-done), kind=kOutput, calls=%fused_computation.8 | convolution fusion | flops 1811939328 | bytes 7077888 | tf_op jit(solution)/shard_map/dot_general | solution.py:60
  88.5 34.7 %all-gather.3.cloned.1.call-done = bf16[1,768,1536]{2,1,0:T(8,128)(2,1)} async-done(((bf16[1,768,384]{2,1,0:T(8,128)(2,1)}), bf16[1,768,1536]{2,1,0:T(8,128)(2,1)}) %all-gather.3.cloned.1.call-update) | async-done | bytes 2359312 | tf_op jit(solution)/shard_map/all_gather | solution.py:57
  123.2 13.3 %all-to-all-done.1 = bf16[8,96,1536]{2,1,0:T(8,128)(2,1)S(1)} async-done(((bf16[8,96,1536]{2,1,0:T(8,128)(2,1)}), bf16[8,96,1536]{2,1,0:T(8,128)(2,1)S(1)}, u32[]{:S(2)}, u32[]{:S(2)}) %all-to-all-start.1) | async-done | bytes 2359328 | tf_op jit(solution)/shard_map/all_to_all | solution.py:61
  136.5 1.5 copy-done
  138.0 8.2 %fusion = bf16[1,1536,768]{2,1,0:T(8,128)(2,1)S(1)} fusion(bf16[768,1536]{1,0:T(8,128)(2,1)} %bitcast.5, f32[768,768]{1,0:T(8,128)} %fusion.2, bf16[768,1536]{1,0:T(8,128)(2,1)} %bitcast.50, bf16[1,768,1536]{2,1,0:T(8,128)(2,1)} %all-gather.3.cloned.1.call-done), kind=kOutput, calls=%fused_computation.5 | convolution fusion | flops 3630366720 | bytes 11796480 | tf_op jit(solution)/shard_map/dot_general | solution.py:14
  146.2 33.8 %copy.24 = bf16[1,1536,768]{2,0,1:T(2,128)(2,1)} copy(bf16[1,1536,768]{2,1,0:T(8,128)(2,1)S(1)} %fusion) | data formatting | bytes 4718592 | tf_op jit(solution)/shard_map/broadcast_in_dim | solution.py:17
  180.5 24.1 %reduce.5 = bf16[1536,768]{1,0:T(8,128)(2,1)S(1)} reduce(bf16[1536,1,768]{2,1,0:T(2,128)(2,1)} %bitcast.47, bf16[]{:T(256)} %broadcast.72), dimensions={1}, to_apply=%bitcast.46.reduce_sub_computation | reduce | bytes 4718594
  204.6 2.2 reshape.129
  206.8 3.7 %all-to-all-start.2 = ((bf16[4,2,147456]{2,1,0:T(2,128)(2,1)}), bf16[4,2,147456]{2,1,0:T(2,128)(2,1)S(1)}, u32[]{:S(2)}, u32[]{:S(2)}) async-start(bf16[4,2,147456]{2,1,0:T(2,128)(2,1)} %reshape.129), calls=%async_computation.2 | async-start | bytes 4718592 | tf_op jit(solution)/shard_map/all_to_all | solution.py:17
  210.5 4.4 %fusion.1 = bf16[1,768,1536]{2,1,0:T(8,128)(2,1)S(1)} fusion(bf16[768,1536]{1,0:T(8,128)(2,1)} %bitcast.51, f32[768,768]{1,0:T(8,128)} %fusion.2), kind=kOutput, calls=%fused_computation.6 | convolution fusion | flops 1816068096 | bytes 7077888 | tf_op jit(solution)/shard_map/dot_general | solution.py:23
  215.2 1.8 pad_maximum_fusion
  217.0 21.0 %all-to-all-done.2 = bf16[4,2,147456]{2,1,0:T(2,128)(2,1)S(1)} async-done(((bf16[4,2,147456]{2,1,0:T(2,128)(2,1)}), bf16[4,2,147456]{2,1,0:T(2,128)(2,1)S(1)}, u32[]{:S(2)}, u32[]{:S(2)}) %all-to-all-start.2) | async-done | bytes 2359328 | tf_op jit(solution)/shard_map/all_to_all | solution.py:17
  238.1 4.5 %all-to-all-start.3 = ((bf16[4,1,768,384]{3,2,1,0:T(8,128)(2,1)}), bf16[4,1,768,384]{3,2,1,0:T(8,128)(2,1)}, u32[]{:S(2)}, u32[]{:S(2)}) async-start(bf16[4,1,768,384]{3,2,1,0:T(8,128)(2,1)} %pad_maximum_fusion), calls=%async_computation.3 | async-start | bytes 4718592 | tf_op jit(solution)/shard_map/all_to_all | solution.py:27
  242.6 3.6 %reshape.130 = bf16[1536,1,768]{2,1,0:T(2,128)(2,1)} reshape(bf16[4,2,147456]{2,1,0:T(2,128)(2,1)S(1)} %all-to-all-done.2) | data formatting | bytes 4718592
  246.1 2.7 copy.22
  250.2 19.6 %all-to-all-done.3 = bf16[4,1,768,384]{3,2,1,0:T(8,128)(2,1)} async-done(((bf16[4,1,768,384]{3,2,1,0:T(8,128)(2,1)}), bf16[4,1,768,384]{3,2,1,0:T(8,128)(2,1)}, u32[]{:S(2)}, u32[]{:S(2)}) %all-to-all-start.3) | async-done | bytes 2359328 | tf_op jit(solution)/shard_map/all_to_all | solution.py:27
  269.8 3.0 %reduce_sum.35 = bf16[768,384]{1,0:T(8,128)(2,1)} reduce(bf16[4,1,768,384]{3,2,1,0:T(8,128)(2,1)} %all-to-all-done.3, bf16[]{:T(256)} %constant.7.clone.1), dimensions={0,1}, to_apply=%region_6.7 | reduce | flops 884736 | bytes 2949122 | tf_op jit(solution)/shard_map/reduce_sum | solution.py:32
  (31 shorter events, 8.0 us)
Async XLA Ops:
  17.1 7.2 %copy-start.1 = (bf16[128,1536]{1,0:T(8,128)(2,1)S(1)}, bf16[128,1536]{1,0:T(8,128)(2,1)}, u32[]{:S(2)}) copy-start(bf16[128,1536]{1,0:T(8,128)(2,1)} %param.7) | copy-start | bytes 1179652
  17.1 61.2 %all-to-all-start = ((bf16[8,96,1536]{2,1,0:T(8,128)(2,1)}), bf16[8,96,1536]{2,1,0:T(8,128)(2,1)}, u32[]{:S(2)}, u32[]{:S(2)}) async-start(bf16[8,96,1536]{2,1,0:T(8,128)(2,1)} %bitcast.4), calls=%async_computation | async-start | bytes 4718592 | tf_op jit(solution)/shard_map/all_to_all | solution.py:58
  23.6 59.2 %all-gather.5.cloned.1.call-start = ((), (), s32[]{:S(2)}) async-start(), calls=%async_computation.5 | async-start | bytes 2949120 | tf_op jit(solution)/shard_map/all_gather | solution.py:56
  24.7 2.3 copy-start.2
  78.3 58.2 %all-to-all-start.1 = ((bf16[8,96,1536]{2,1,0:T(8,128)(2,1)}), bf16[8,96,1536]{2,1,0:T(8,128)(2,1)S(1)}, u32[]{:S(2)}, u32[]{:S(2)}) async-start(bf16[8,96,1536]{2,1,0:T(8,128)(2,1)} %bitcast.6), calls=%async_computation.1 | async-start | bytes 4718592 | tf_op jit(solution)/shard_map/all_to_all | solution.py:61
  82.0 41.3 %all-gather.3.cloned.1.call-start = ((), (), s32[]{:S(2)}) async-start(), calls=%async_computation.4 | async-start | bytes 2949120 | tf_op jit(solution)/shard_map/all_gather | solution.py:57
  136.5 1.5 copy-start
  206.8 31.3 %all-to-all-start.2 = ((bf16[4,2,147456]{2,1,0:T(2,128)(2,1)}), bf16[4,2,147456]{2,1,0:T(2,128)(2,1)S(1)}, u32[]{:S(2)}, u32[]{:S(2)}) async-start(bf16[4,2,147456]{2,1,0:T(2,128)(2,1)} %reshape.129), calls=%async_computation.2 | async-start | bytes 4718592 | tf_op jit(solution)/shard_map/all_to_all | solution.py:17
  238.1 31.7 %all-to-all-start.3 = ((bf16[4,1,768,384]{3,2,1,0:T(8,128)(2,1)}), bf16[4,1,768,384]{3,2,1,0:T(8,128)(2,1)}, u32[]{:S(2)}, u32[]{:S(2)}) async-start(bf16[4,1,768,384]{3,2,1,0:T(8,128)(2,1)} %pad_maximum_fusion), calls=%async_computation.3 | async-start | bytes 4718592 | tf_op jit(solution)/shard_map/all_to_all | solution.py:27
Sparse Core Ops, SparseCore 0:
  26.2 38.7 all-gather.4
  84.6 38.5 all-gather.2
